TPU v7x, 32 devices: a whole 2x2x4 slice. The times are simulated.
32 devices in a mesh: crop: 2 (over x), row: 8 (over z, y), col: 2 (over core).
Axes of the slice: x: 2, y: 2, z: 4, core: 2. Of those that a mesh axis runs over, the one named last changes fastest.
Arguments:
- pair_rep: bfloat16 [96, 48, 128], P(('crop', 'row'), 'col'), parts along dimension 0, may hold values from -6 to 6
- cotangent: bfloat16 [96, 48, 128], P(('crop', 'row'), 'col'), parts along dimension 0, may hold values from -6 to 6
- norm_gain: float32 [128], replicated, may hold values from 0.5 to 1.5
- norm_bias: float32 [128], replicated, may hold values from -3 to 3
- proj_weight: bfloat16 [128, 512], replicated, may hold values from -0.5 to 0.5
- gate_weight: bfloat16 [128, 128], replicated, may hold values from -0.5 to 0.5
- tri_gain: float32 [128], replicated, may hold values from 0.5 to 1.5
- tri_bias: float32 [128], replicated, may hold values from -3 to 3
- out_weight: bfloat16 [128, 128], replicated, may hold values from -0.5 to 0.5
Outputs:
- block_out: bfloat16 [96, 48, 128], P(('crop', 'row'), 'col'), parts along dimension 0
- pair_grad: float32 [96, 48, 128], P(('crop', 'row'), 'col'), parts along dimension 0
- proj_grad: float32 [256, 512], P('crop'), parts along dimension 0
- gate_grad: float32 [256, 128], P('crop'), parts along dimension 0
- out_grad: float32 [256, 128], P('crop'), parts along dimension 0
There are 2 independent parts, one for each index of `crop`. A program takes and returns all parts, laid end to end along the dimension named above; an argument that names none is the same for every part. Nothing has to cross between parts.
All inputs are finite; a program needn't handle non-finite values.
Results may differ from a plain program's by a relative error of at most 0.0066.
Values may be sent and summed in bfloat16 or wider, within the bound.
A program may use at most 128 MiB of HBM per device.

v0:
```python
import jax
import jax.numpy as jnp
from jax import lax
from jax.sharding import PartitionSpec as P


def layer_norm(values, gain, bias):
    centred = values - jnp.mean(values, axis=-1, keepdims=True)
    inverse = lax.rsqrt(jnp.mean(centred * centred, axis=-1, keepdims=True) + 1e-05)
    scaled = centred * inverse
    return (scaled * gain + bias, scaled, inverse)


def norm_back(grads, gain, scaled, inverse):
    weighted = grads * gain
    first = jnp.mean(weighted, axis=-1, keepdims=True)
    second = jnp.mean(weighted * scaled, axis=-1, keepdims=True)
    return inverse * (weighted - first - scaled * second)


def local(
    pair_rep,
    cotangent,
    norm_gain,
    norm_bias,
    proj_weight,
    gate_weight,
    tri_gain,
    tri_bias,
    out_weight,
):
    f32 = jnp.float32
    bf16 = jnp.bfloat16
    hidden = tri_gain.shape[0]
    channels = norm_gain.shape[0]
    row_count = pair_rep.shape[0]
    col_count = pair_rep.shape[1]
    crop_len = row_count * lax.axis_size("row")
    normed_f, pair_hat, pair_inv = layer_norm(pair_rep.astype(f32), norm_gain, norm_bias)
    normed = normed_f.astype(bf16)
    projected = jnp.einsum("ijc,cd->ijd", normed, proj_weight, preferred_element_type=f32)
    sig_left = jax.nn.sigmoid(projected[..., 0:hidden])
    val_left = projected[..., hidden : 2 * hidden]
    sig_right = jax.nn.sigmoid(projected[..., 2 * hidden : 3 * hidden])
    val_right = projected[..., 3 * hidden : 4 * hidden]
    left_edge = (sig_left * val_left).astype(bf16)
    right_edge = (sig_right * val_right).astype(bf16)
    out_gate = jax.nn.sigmoid(
        jnp.einsum("ijc,cd->ijd", normed, gate_weight, preferred_element_type=f32)
    )
    right_all = lax.all_gather(right_edge, "row", axis=0, tiled=True)
    block = right_all
    triangle = lax.psum_scatter(
        jnp.einsum("ikc,jkc->jic", left_edge, block, preferred_element_type=f32),
        "col",
        scatter_dimension=0,
        tiled=True,
    ).transpose(1, 0, 2)
    tri_f, tri_hat, tri_inv = layer_norm(triangle, tri_gain, tri_bias)
    tri_norm = tri_f.astype(bf16)
    update = jnp.einsum("ijh,hc->ijc", tri_norm, out_weight, preferred_element_type=f32)
    block_out = (out_gate * update).astype(bf16)
    cot = cotangent.astype(f32)
    d_update = (cot * out_gate).astype(bf16)
    d_gate = (cot * update * out_gate * (1.0 - out_gate)).astype(bf16)
    d_norm = jnp.einsum("ijc,hc->ijh", d_update, out_weight, preferred_element_type=f32)
    d_triangle = norm_back(d_norm, tri_gain, tri_hat, tri_inv).astype(bf16)
    tri_rows = lax.all_gather(d_triangle, "col", axis=1, tiled=True)
    d_left = jnp.einsum("ijc,jkc->ikc", tri_rows, right_all, preferred_element_type=f32)
    tri_cols = lax.all_to_all(tri_rows, "row", split_axis=1, concat_axis=0, tiled=True)
    block = tri_cols
    d_right = jnp.einsum(
        "ijc,ikc->jkc",
        block,
        lax.all_gather(left_edge, "row", axis=0, tiled=True),
        preferred_element_type=f32,
    )
    d_proj = jnp.concatenate(
        [
            d_left * val_left * sig_left * (1.0 - sig_left),
            d_left * sig_left,
            d_right * val_right * sig_right * (1.0 - sig_right),
            d_right * sig_right,
        ],
        axis=-1,
    ).astype(bf16)
    d_normed = jnp.einsum(
        "ijd,cd->ijc", d_proj, proj_weight, preferred_element_type=f32
    ) + jnp.einsum("ijd,cd->ijc", d_gate, gate_weight, preferred_element_type=f32)
    pair_grad = norm_back(d_normed, norm_gain, pair_hat, pair_inv)
    cells = row_count * col_count
    flat_norm = normed.reshape(cells, channels)
    local_proj = (
        jnp.dot(flat_norm.T, d_proj.reshape(cells, 4 * hidden), preferred_element_type=f32)
        / crop_len
    )
    local_gate = (
        jnp.dot(flat_norm.T, d_gate.reshape(cells, channels), preferred_element_type=f32) / crop_len
    )
    local_out = (
        jnp.dot(
            tri_norm.reshape(cells, hidden).T,
            d_update.reshape(cells, channels),
            preferred_element_type=f32,
        )
        / crop_len
    )
    proj_grad, gate_grad, out_grad = lax.psum((local_proj, local_gate, local_out), ("row", "col"))
    return (block_out, pair_grad, proj_grad, gate_grad, out_grad)


def solution(mesh):
    return jax.shard_map(
        local,
        mesh=mesh,
        in_specs=(
            P(("crop", "row"), "col", None),
            P(("crop", "row"), "col", None),
            P(),
            P(),
            P(),
            P(),
            P(),
            P(),
            P(),
        ),
        out_specs=(
            P(("crop", "row"), "col", None),
            P(("crop", "row"), "col", None),
            P("crop", None),
            P("crop", None),
            P("crop", None),
        ),
        check_vma=False,
    )
```

profile of v0, /device:TPU:0, one launch (start us, length us, event | category | flops | bytes accessed | tf_op | source)
XLA Modules:
  0.0 211.7 jit_solution(7040037834363857959)
XLA Ops:
  7.2 0.9 convert_reduce_fusion
  8.1 0.9 fusion.21
  9.1 1.0 fusion.9
  10.2 0.6 copy-done.2
  10.8 32.6 %all_gather.9 = bf16[48,24,128]{2,1,0:T(8,128)(2,1)S(1)} all-gather(bf16[6,24,128]{2,1,0:T(8,128)(2,1)S(1)} %get-tuple-element.19), channel_id=1, replica_groups=mesh['crop'=2,'row'=8,'col'=2] {'row'}, dimensions={0}, use_global_device_ids=true | all-gather | bytes 331776 | tf_op jit(solution)/shard_map/all_gather | solution.py:51
  43.4 0.9 copy.36
  44.6 0.9 convolution_bitcast_fusion
  45.5 0.9 copy.38
  46.4 32.9 %all_gather.11 = bf16[48,24,128]{2,1,0:T(8,128)(2,1)} all-gather(bf16[6,24,128]{2,1,0:T(8,128)(2,1)S(1)} %get-tuple-element.18), channel_id=1, replica_groups=mesh['crop'=2,'row'=8,'col'=2] {'row'}, dimensions={0}, use_global_device_ids=true | all-gather | bytes 331776 | tf_op jit(solution)/shard_map/all_gather | solution.py:75
  79.4 1.8 copy.46
  81.2 1.0 bitcast_reduce_fusion
  82.2 1.1 multiply_reduce_fusion.1
  83.3 1.1 fusion.42
  84.4 1.6 fusion.25
  86.1 1.2 fusion.55
  87.3 1.0 multiply_convert_fusion
  88.3 1.9 all_gather.10
  90.2 0.9 copy.41
  91.1 0.7 copy.43
  91.7 2.3 %fusion.56 = f32[128,24,6]{1,2,0:T(8,128)} fusion(bf16[48,24,128]{1,0,2:T(8,128)(2,1)S(1)} %copy.36, bf16[6,48,128]{1,0,2:T(8,128)(2,1)} %copy.41), kind=kOutput, calls=%fused_computation.85 | convolution fusion | flops 1769472 | bytes 442368 | tf_op jit(solution)/shard_map/ijc,jkc->ikc/dot_general | solution.py:69
  94.0 1.2 copy.42
  95.2 5.6 %all-to-all-start = ((bf16[6,48,128]{2,0,1:T(8,128)(2,1)}), bf16[6,48,128]{2,0,1:T(8,128)(2,1)S(1)}, u32[]{:S(2)}, u32[]{:S(2)}) async-start(bf16[6,48,128]{2,0,1:T(8,128)(2,1)} %copy.43), calls=%async_computation.1 | async-start | bytes 196608 | tf_op jit(solution)/shard_map/all_to_all | solution.py:70
  100.9 0.9 fusion.5
  101.8 1.7 fusion.6
  103.5 4.5 %all-to-all-done = bf16[6,48,128]{2,0,1:T(8,128)(2,1)S(1)} async-done(((bf16[6,48,128]{2,0,1:T(8,128)(2,1)}), bf16[6,48,128]{2,0,1:T(8,128)(2,1)S(1)}, u32[]{:S(2)}, u32[]{:S(2)}) %all-to-all-start) | async-done | bytes 73760 | tf_op jit(solution)/shard_map/all_to_all | solution.py:70
  108.2 0.5 fusion.57
  109.2 1.0 fusion
  110.6 0.8 fusion.20
  111.4 88.9 %all-reduce.3.cloned.1.call-done = (f32[128,512]{1,0:T(8,128)}, f32[128,128]{1,0:T(8,128)}, f32[128,128]{1,0:T(8,128)}) async-done(((f32[128,512]{1,0:T(8,128)}, f32[128,128]{1,0:T(8,128)}, f32[128,128]{1,0:T(8,128)}), (f32[128,512]{1,0:T(8,128)}, f32[128,128]{1,0:T(8,128)}, f32[128,128]{1,0:T(8,128)})) %all-reduce.3.cloned.1.call-update) | async-done | bytes 393232 | tf_op jit(solution)/shard_map/psum | solution.py:108
  200.2 1.7 copy.61
  201.9 1.5 copy.62
  203.4 1.5 copy.63
  (46 shorter events, 1.5 us)
Async XLA Ops:
  7.2 1.9 copy-start
  7.2 74.0 %reduce-scatter.2.cloned.1.call-start = ((), (), s32[]{:S(2)}) async-start(), calls=%async_computation.2 | async-start | bytes 294912 | tf_op jit(solution)/shard_map/reduce_scatter | solution.py:53
  10.1 0.7 copy-start.2
  45.5 37.8 %copy-start.6 = (bf16[128,128]{1,0:T(8,128)(2,1)S(1)}, bf16[128,128]{1,0:T(8,128)(2,1)}, u32[]{:S(2)}) copy-start(bf16[128,128]{1,0:T(8,128)(2,1)} %param.17) | copy-start | bytes 98308
  45.5 37.8 %copy-start.9 = (f32[128]{0:T(128)S(1)}, f32[128]{0:T(128)}, u32[]{:S(2)}) copy-start(f32[128]{0:T(128)} %param.15) | copy-start | bytes 1540
  45.5 37.8 %copy-start.10 = (f32[128]{0:T(128)S(1)}, f32[128]{0:T(128)}, u32[]{:S(2)}) copy-start(f32[128]{0:T(128)} %param.16) | copy-start | bytes 1540
  46.4 38.0 %copy-start.4 = (bf16[6,24,128]{2,1,0:T(8,128)(2,1)S(1)}, bf16[6,24,128]{2,1,0:T(8,128)(2,1)}, u32[]{:S(2)}) copy-start(bf16[6,24,128]{2,1,0:T(8,128)(2,1)} %param.9) | copy-start | bytes 110596
  46.4 38.0 %copy-start.5 = (bf16[6,24,128]{2,1,0:T(8,128)(2,1)S(1)}, bf16[6,24,128]{2,1,0:T(8,128)(2,1)}, u32[]{:S(2)}) copy-start(bf16[6,24,128]{2,1,0:T(8,128)(2,1)} %param.10) | copy-start | bytes 110596
  46.4 38.0 %copy-start.11 = (f32[128]{0:T(128)S(1)}, f32[128]{0:T(128)}, u32[]{:S(2)}) copy-start(f32[128]{0:T(128)} %param.11) | copy-start | bytes 1540
  46.4 38.0 %copy-start.12 = (f32[128]{0:T(128)S(1)}, f32[128]{0:T(128)}, u32[]{:S(2)}) copy-start(f32[128]{0:T(128)} %param.12) | copy-start | bytes 1540
  91.7 9.1 %copy-start.1 = (f32[24,6,128]{2,1,0:T(8,128)S(1)}, f32[24,6,128]{2,1,0:T(8,128)}, u32[]{:S(2)}) copy-start(f32[24,6,128]{2,1,0:T(8,128)} %reduce-scatter.2.cloned.1.call-done) | copy-start | bytes 221188
  95.2 12.7 %all-to-all-start = ((bf16[6,48,128]{2,0,1:T(8,128)(2,1)}), bf16[6,48,128]{2,0,1:T(8,128)(2,1)S(1)}, u32[]{:S(2)}, u32[]{:S(2)}) async-start(bf16[6,48,128]{2,0,1:T(8,128)(2,1)} %copy.43), calls=%async_computation.1 | async-start | bytes 196608 | tf_op jit(solution)/shard_map/all_to_all | solution.py:70
  100.8 99.4 %all-reduce.3.cloned.1.call-start = ((), (), s32[]{:S(2)}) async-start(), calls=%async_computation.3 | async-start | bytes 786432 | tf_op jit(solution)/shard_map/psum | solution.py:108
  108.0 1.0 copy-start.3
  108.7 1.5 copy-start.7
  108.7 1.5 copy-start.8
Sparse Core Ops, SparseCore 0:
  46.5 8.6 reduce-scatter.1
  110.7 89.4 all-reduce.2
where the time goes:
time: 213 us; the launch traced here: 212 us
  waiting for transfers between devices  93.4 us (44%)
  blocking collectives  67.4 us (32%)
  between operations  14.3 us (7%)
  matrix products  12.8 us (6%)
  local copies, waits for them, and re-layouts  12.3 us (6%)
  other arithmetic  5.82 us (3%)
  starting transfers between devices  5.68 us (3%)
    psum x1, waiting for transfers between devices, local(): lax.psum((local_proj, local_gate, local_out), ('row', 'col'))  88.9 us
    all_gather x1, blocking collectives, local(): lax.all_gather(left_edge, 'row', axis=0, tiled=True)  32.9 us
    all_gather x1, blocking collectives, local(): right_all = lax.all_gather(right_edge, 'row', axis=0, tiled=True)  32.6 us
    all_to_all x1, starting transfers between devices, local(): lax.all_to_all(tri_rows, 'row', split_axis=1, concat_axis=0, tiled=True)  5.6 us
    unnamed x29, local copies, waits for them, and re-layouts  5.38 us
    all_to_all x1, waiting for transfers between devices, local(): lax.all_to_all(tri_rows, 'row', split_axis=1, concat_axis=0, tiled=True)  4.46 us
  transfers between devices with their start and end apart: 3, of which 2 were waited for; matrix products, arithmetic and copies ran while one was open for 2% of the time, Pallas kernels for 0%

commit v1 on v0

v1 whole, which is shorter than its diff:
```python
import functools

import jax
import jax.numpy as jnp
from jax import lax
from jax.experimental import pallas as pl
from jax.experimental.pallas import tpu as pltpu
from jax.sharding import PartitionSpec as P

F32 = jnp.float32
BF16 = jnp.bfloat16


def mean_last(values):
    return jnp.mean(values, axis=-1, keepdims=True)


def normalise(values):
    centred = values - mean_last(values)
    inverse = lax.rsqrt(mean_last(centred * centred) + 1e-05)
    return centred * inverse, inverse


def norm_back(weighted, scaled, inverse):
    return inverse * (weighted - mean_last(weighted) - scaled * mean_last(weighted * scaled))


def dot(a, b, ca=1, cb=0):
    return lax.dot_general(a, b, (((ca,), (cb,)), ((), ())), preferred_element_type=F32)


def kernel(
    R, Q, rows, K, H, C,
    x_ref, cot_ref, ng_ref, nb_ref, pw_ref, gw_ref, tg_ref, tb_ref, ow_ref,
    out_ref, pg_ref, gp_ref, gg_ref, go_ref,
    edges, right32, left32, coef, og_s, hat_s, inv_s, normed_s, dupd_s, dnorm_s,
    tri_s, tri_rcv, d32, drow, drow32, dsend, drecv, dcol32, tnorm_s, dgate_s,
    g32, gsend, grecv, gfin,
    edge_ss, edge_rs, tri_ss, tri_rs, drow_ss, drow_rs, dcol_ss, dcol_rs,
    gs_ss, gs_rs, gf_ss, gf_rs,
):
    r = lax.axis_index("row")
    q = lax.axis_index("col")
    M = rows * K
    N = rows * R
    NP = R * Q
    RPQ = R // Q
    pad = -(-rows // 8) * 8
    me = r * Q + q

    def remote(src, dst, ss, rs, rr, qq):
        return pltpu.make_async_remote_copy(
            src_ref=src, dst_ref=dst, send_sem=ss, recv_sem=rs,
            device_id={"row": rr, "col": qq}, device_id_type=pl.DeviceIdType.MESH,
        )

    def loop(lo, hi, body):
        def step(t, carry):
            body(t)
            return carry
        lax.fori_loop(lo, hi, step, 0, unroll=(hi - lo) <= 16)

    barrier = pltpu.get_barrier_semaphore()

    def greet(t):
        other = lax.rem(me + t, NP)
        pl.semaphore_signal(
            barrier, inc=1,
            device_id={"row": other // Q, "col": lax.rem(other, Q)},
            device_id_type=pl.DeviceIdType.MESH,
        )

    loop(1, NP, greet)

    hat, inv = normalise(x_ref[...].astype(F32))
    normed = (hat * ng_ref[...] + nb_ref[...]).astype(BF16)
    hat_s[...] = hat
    inv_s[...] = jnp.broadcast_to(inv, hat.shape)
    normed_s[...] = normed
    right = dot(normed, pw_ref[:, 2 * H :])
    sr = jax.nn.sigmoid(right[:, :H])
    vr = right[:, H:]
    right_edge = (sr * vr).astype(BF16)
    edges[0, r] = right_edge
    left = dot(normed, pw_ref[:, : 2 * H])
    sl = jax.nn.sigmoid(left[:, :H])
    vl = left[:, H:]
    left_edge = (sl * vl).astype(BF16)
    edges[1, r] = left_edge

    pl.semaphore_wait(barrier, NP - 1)

    for side in range(2):
        def send(t, side=side):
            other = lax.rem(r + t, R)
            remote(
                edges.at[side, r], edges.at[side, r], edge_ss.at[side, t], edge_rs.at[side, r],
                other, q,
            ).start()
        loop(1, R, send)

    def edge_wait(side):
        def wait(t):
            other = lax.rem(r + R - t, R)
            remote(
                edges.at[side, r], edges.at[side, other], edge_ss.at[side, t],
                edge_rs.at[side, other], other, q,
            ).wait_recv()
        loop(1, R, wait)

    own = pl.multiple_of(r * M, 8)
    left32[pl.ds(own, M), :] = left_edge.astype(F32)
    coef[0] = vl * sl * (1.0 - sl)
    coef[1] = sl
    coef[2] = vr * sr * (1.0 - sr)
    coef[3] = sr
    og = jax.nn.sigmoid(dot(normed, gw_ref[...]))
    og_s[...] = og
    d_update = (cot_ref[...].astype(F32) * og).astype(BF16)
    dupd_s[...] = d_update
    dnorm_s[...] = dot(d_update, ow_ref[...], 1, 1) * tg_ref[...]

    edge_wait(0)

    def widen_right(t):
        right32[pl.ds(pl.multiple_of(t * M, 8), M), :] = edges[0, t].astype(F32)
    loop(0, R, widen_right)

    def partial(half):
        base = half * (K * K)

        def step(k, accs):
            block = right32[pl.ds(base + k, K, stride=K), :]
            return tuple(
                accs[i] + left32[pl.ds(own + i * K + k, 1), :] * block for i in range(rows)
            )
        accs = lax.fori_loop(
            0, K, step, tuple(jnp.zeros((K, H), F32) for _ in range(rows)), unroll=4
        )
        for i in range(rows):
            tri_s[half, i * K : (i + 1) * K, :] = accs[i]

    for t in range(1, Q):
        other = lax.rem(q + t, Q)
        partial(other)
        remote(
            tri_s.at[other], tri_rcv.at[q], tri_ss.at[t], tri_rs.at[q], r, other
        ).start()
    partial(q)
    triangle = tri_s[q]
    for t in range(1, Q):
        other = lax.rem(q + Q - t, Q)
        remote(
            tri_s.at[other], tri_rcv.at[other], tri_ss.at[t], tri_rs.at[other], r, other
        ).wait_recv()
        triangle = triangle + tri_rcv[other]

    tri_hat, tri_inv = normalise(triangle)
    d_tri = norm_back(dnorm_s[...], tri_hat, tri_inv).astype(BF16)
    drow[q] = d_tri
    for t in range(1, Q):
        other = lax.rem(q + t, Q)
        remote(drow.at[q], drow.at[q], drow_ss.at[t], drow_rs.at[q], r, other).start()
    d_tri32 = d_tri.astype(F32)
    d32[...] = d_tri32
    for b in range(RPQ):
        parts = []
        for i in range(rows):
            piece = d32[i * K + b * rows : i * K + (b + 1) * rows, :]
            if pad > rows:
                piece = jnp.concatenate([piece, jnp.zeros((pad - rows, H), F32)], axis=0)
            parts.append(piece)
        dsend[b] = jnp.concatenate(parts, axis=0).astype(BF16)

    def each_target(act):
        for t in range(Q):
            def one(b, t=t):
                target = q * RPQ + b
                other = lax.rem(q + t, Q)
                if t:
                    act(b, t, target, other)
                else:
                    @pl.when(target != r)
                    def _():
                        act(b, t, target, other)
            loop(0, RPQ, one)

    def col_copy(b, t, target, other):
        return remote(
            dsend.at[b], drecv.at[r], dcol_ss.at[t * RPQ + b], dcol_rs.at[r], target, other
        )

    each_target(lambda b, t, target, other: col_copy(b, t, target, other).start())
    mine = r // RPQ == q

    @pl.when(mine)
    def _():
        drecv[r] = dsend[lax.rem(r, RPQ)]

    tri_norm = (tri_hat * tg_ref[...] + tb_ref[...]).astype(BF16)
    update = dot(tri_norm, ow_ref[...])
    og = og_s[...]
    out_ref[...] = (og * update).astype(BF16)
    d_gate = (cot_ref[...].astype(F32) * update * og * (1.0 - og)).astype(BF16)
    dgate_s[...] = d_gate
    g32[4 * C : 5 * C, :] = dot(normed_s[...], d_gate, 0, 0)
    g32[5 * C : 6 * C, :] = dot(tri_norm, dupd_s[...], 0, 0)

    drow32[pl.ds(pl.multiple_of(q * M, 8), M), :] = d_tri32
    for t in range(1, Q):
        other = lax.rem(q + Q - t, Q)
        remote(
            drow.at[q], drow.at[other], drow_ss.at[t], drow_rs.at[other], r, other
        ).wait_recv()
        drow32[pl.ds(pl.multiple_of(other * M, 8), M), :] = drow[other].astype(F32)

    def zeros():
        return tuple(jnp.zeros((K, H), F32) for _ in range(rows))

    accs = zeros()
    for h in range(Q):
        def left_step(j, accs, h=h):
            block = right32[pl.ds(pl.multiple_of((h * K + j) * K, 8), K), :]
            return tuple(
                accs[i] + drow32[pl.ds(h * M + i * K + j, 1), :] * block for i in range(rows)
            )
        accs = lax.fori_loop(0, K, left_step, accs, unroll=4)
    d_left = jnp.concatenate(accs, axis=0)
    d_proj = [(d_left * coef[0]).astype(BF16), (d_left * coef[1]).astype(BF16)]

    edge_wait(1)

    def widen_left(t):
        left32[pl.ds(pl.multiple_of(t * M, 8), M), :] = edges[1, t].astype(F32)
    loop(0, R, widen_left)

    owner = r // RPQ

    def col_wait(t):
        source = lax.rem(r + R - t, R)
        remote(
            dsend.at[0], drecv.at[source], dcol_ss.at[0], dcol_rs.at[source], source, owner
        ).wait_recv()
    loop(1, R, col_wait)

    @pl.when(jnp.logical_not(mine))
    def _():
        remote(dsend.at[0], drecv.at[r], dcol_ss.at[0], dcol_rs.at[r], r, owner).wait_recv()

    def widen_col(t):
        dcol32[pl.ds(pl.multiple_of(t * rows * pad, 8), rows * pad), :] = drecv[t].astype(F32)
    loop(0, R, widen_col)

    def right_step(i, accs):
        block = left32[pl.ds(pl.multiple_of(i * K, 8), K), :]
        return tuple(
            accs[j] + dcol32[pl.ds(i * pad + j, 1), :] * block for j in range(rows)
        )
    d_right = jnp.concatenate(lax.fori_loop(0, N, right_step, zeros(), unroll=4), axis=0)
    d_proj += [(d_right * coef[2]).astype(BF16), (d_right * coef[3]).astype(BF16)]

    for b in range(4):
        g32[b * C : (b + 1) * C, :] = dot(normed_s[...], d_proj[b], 0, 0)
    piece = 6 * C // NP
    for p in range(NP):
        gsend[p] = g32[p * piece : (p + 1) * piece, :].astype(BF16)

    def scatter(t):
        other = lax.rem(me + t, NP)
        return remote(
            gsend.at[other], grecv.at[me], gs_ss.at[t], gs_rs.at[me],
            other // Q, lax.rem(other, Q),
        )
    loop(1, NP, lambda t: scatter(t).start())
    grecv[me] = gsend[me]

    d_cat = jnp.concatenate(d_proj, axis=-1)
    d_normed = dot(d_cat, pw_ref[...], 1, 1) + dot(dgate_s[...], gw_ref[...], 1, 1)
    pg_ref[...] = norm_back(d_normed * ng_ref[...], hat_s[...], inv_s[...])

    def scatter_wait(t):
        other = lax.rem(me + NP - t, NP)
        remote(
            gsend.at[0], grecv.at[other], gs_ss.at[t], gs_rs.at[other],
            other // Q, lax.rem(other, Q),
        ).wait_recv()
    loop(1, NP, scatter_wait)
    total = grecv[0].astype(F32)
    for p in range(1, NP):
        total = total + grecv[p].astype(F32)
    gfin[me] = (total / N).astype(BF16)

    def spread(t):
        other = lax.rem(me + t, NP)
        return remote(
            gfin.at[me], gfin.at[me], gf_ss.at[t], gf_rs.at[me],
            other // Q, lax.rem(other, Q),
        )
    loop(1, NP, lambda t: spread(t).start())

    for side in range(2):
        loop(1, R, lambda t, side=side: remote(
            edges.at[side, r], edges.at[side, r], edge_ss.at[side, t], edge_rs.at[side, r], r, q
        ).wait_send())
    for t in range(1, Q):
        other = lax.rem(q + t, Q)
        remote(tri_s.at[other], tri_rcv.at[q], tri_ss.at[t], tri_rs.at[q], r, other).wait_send()
        remote(drow.at[q], drow.at[q], drow_ss.at[t], drow_rs.at[q], r, other).wait_send()
    each_target(lambda b, t, target, other: col_copy(b, t, target, other).wait_send())
    loop(1, NP, lambda t: scatter(t).wait_send())

    def spread_wait(t):
        other = lax.rem(me + NP - t, NP)
        remote(
            gfin.at[me], gfin.at[other], gf_ss.at[t], gf_rs.at[other],
            other // Q, lax.rem(other, Q),
        ).wait_recv()
    loop(1, NP, spread_wait)
    for p in range(NP):
        g32[p * piece : (p + 1) * piece, :] = gfin[p].astype(F32)
    for b in range(4):
        gp_ref[:, b * H : (b + 1) * H] = g32[b * C : (b + 1) * C, :]
    gg_ref[...] = g32[4 * C : 5 * C, :]
    go_ref[...] = g32[5 * C : 6 * C, :]
    loop(1, NP, lambda t: spread(t).wait_send())


def local(R, Q, pair_rep, cotangent, ng, nb, pw, gw, tg, tb, ow):
    rows, K, C = pair_rep.shape
    H = tg.shape[0]
    M = rows * K
    NP = R * Q
    RPQ = R // Q
    pad = -(-rows // 8) * 8
    piece = 6 * C // NP
    dma = pltpu.SemaphoreType.DMA
    vmem = pltpu.VMEM
    spec = pl.BlockSpec(memory_space=pltpu.VMEM)
    shapes = (
        jax.ShapeDtypeStruct((M, C), BF16),
        jax.ShapeDtypeStruct((M, C), F32),
        jax.ShapeDtypeStruct((C, 4 * H), F32),
        jax.ShapeDtypeStruct((C, C), F32),
        jax.ShapeDtypeStruct((H, C), F32),
    )
    outs = pl.pallas_call(
        functools.partial(kernel, R, Q, rows, K, H, C),
        out_shape=shapes,
        in_specs=[spec] * 9,
        out_specs=[spec] * 5,
        scratch_shapes=[
            vmem((2, R, M, H), BF16),
            vmem((R * M, H), F32),
            vmem((R * M, H), F32),
            vmem((4, M, H), F32),
            vmem((M, C), F32),
            vmem((M, C), F32),
            vmem((M, C), F32),
            vmem((M, C), BF16),
            vmem((M, C), BF16),
            vmem((M, H), F32),
            vmem((Q, M, H), F32),
            vmem((Q, M, H), F32),
            vmem((M, H), F32),
            vmem((Q, M, H), BF16),
            vmem((Q * M, H), F32),
            vmem((RPQ, rows * pad, H), BF16),
            vmem((R, rows * pad, H), BF16),
            vmem((R * rows * pad, H), F32),
            vmem((M, H), BF16),
            vmem((M, C), BF16),
            vmem((6 * C, H), F32),
            vmem((NP, piece, H), BF16),
            vmem((NP, piece, H), BF16),
            vmem((NP, piece, H), BF16),
            dma((2, R)), dma((2, R)),
            dma((Q,)), dma((Q,)),
            dma((Q,)), dma((Q,)),
            dma((R,)), dma((R,)),
            dma((NP,)), dma((NP,)),
            dma((NP,)), dma((NP,)),
        ],
        compiler_params=pltpu.CompilerParams(
            collective_id=0, has_side_effects=True, vmem_limit_bytes=60 * 1024 * 1024
        ),
        name="triangle_step",
    )(
        pair_rep.reshape(M, C), cotangent.reshape(M, C), ng.reshape(1, C), nb.reshape(1, C),
        pw, gw, tg.reshape(1, H), tb.reshape(1, H), ow,
    )
    return (
        outs[0].reshape(rows, K, C), outs[1].reshape(rows, K, C), outs[2], outs[3], outs[4],
    )


def solution(mesh):
    tile = P(("crop", "row"), "col", None)
    grad = P("crop", None)
    return jax.shard_map(
        functools.partial(local, mesh.shape["row"], mesh.shape["col"]),
        mesh=mesh,
        in_specs=(tile, tile, P(), P(), P(), P(), P(), P(), P()),
        out_specs=(tile, tile, grad, grad, grad),
        check_vma=False,
    )
```

time: 213 us -> 42.7 us (0.20)
  waiting for transfers between devices: 93.4 us -> 0 us
  blocking collectives: 67.4 us -> 0 us
  Pallas kernels: 0 us -> 36.5 us
  between operations: 14.3 us -> 0.66 us
  matrix products: 12.8 us -> 0 us
  local copies, waits for them, and re-layouts: 12.3 us -> 5.25 us
  other arithmetic: 5.82 us -> 0 us
  starting transfers between devices: 5.68 us -> 0 us
    psum x1 -> x0, waiting for transfers between devices: 88.9 us -> none  [local(): lax.psum((local_proj, local_gate, local_out), ('row', 'col'))]
    all_gather x3 -> x0, blocking collectives: 67.4 us -> none  [the longest x1 32.9 us: local(): lax.all_gather(left_edge, 'row', axis=0, tiled=True)]
    pallas_call x0 -> x1, Pallas kernels: none -> 36.5 us  [local(): pl.pallas_call(functools.partial(kernel, R, Q, rows, K, H, C), out_shape=...]
    dot_general x12 -> x0, matrix products: 12.8 us -> none  [the longest x1 2.29 us: local(): jnp.einsum('ijc,jkc->ikc', tri_rows, right_all, preferred_element_type=f32)]
    all_to_all x1 -> x0, starting transfers between devices: 5.6 us -> none  [local(): lax.all_to_all(tri_rows, 'row', split_axis=1, concat_axis=0, tiled=True)]
    all_to_all x1 -> x0, waiting for transfers between devices: 4.46 us -> none  [local(): lax.all_to_all(tri_rows, 'row', split_axis=1, concat_axis=0, tiled=True)]
    all_gather x4 -> x0, local copies, waits for them, and re-layouts: 4.28 us -> none  [the longest x1 1.79 us: local(): lax.all_gather(left_edge, 'row', axis=0, tiled=True)]
    reduce_sum x4 -> x0, other arithmetic: 3.85 us -> none  [the longest x2 1.98 us: layer_norm(): jnp.mean(centred * centred, axis=-1, keepdims=True) + 1e-05]
  transfers between devices with their start and end apart: 3 -> 0, of which waited for: 2 -> 0; matrix products, arithmetic and copies ran while one was open for 2% -> 0% of each run, Pallas kernels for 0% -> 0%
where the time goes in v1:
time: 42.7 us; the launch traced here: 42.4 us
  Pallas kernels  36.5 us (85%)
  local copies, waits for them, and re-layouts  5.25 us (12%)
  between operations  0.66 us (2%)
    pallas_call x1, Pallas kernels, local(): pl.pallas_call(functools.partial(kernel, R, Q, rows, K, H, C), out_shape=...  36.5 us
    unnamed x11, local copies, waits for them, and re-layouts  5.25 us

profile of v1, /device:TPU:0, one launch (start us, length us, event | category | flops | bytes accessed | tf_op | source)
XLA Modules:
  0.0 42.4 jit_solution(9046656594752865594)
XLA Ops:
  0.6 36.5 %triangle_step.1 = (bf16[144,128]{1,0:T(8,128)(2,1)}, f32[144,128]{1,0:T(8,128)}, f32[128,512]{1,0:T(8,128)}, f32[128,128]{1,0:T(8,128)}, f32[128,128]{1,0:T(8,128)}) custom-call(bf16[144,128]{1,0:T(8,128)(2,1)} %bitcast.10, bf16[144,128]{1,0:T(8,128)(2,1)} %bitcast.11, f32[1,128]{1,0:T(1,128)} %bitcast.12, f32[1,128]{1,0:T(1,128)} %bitcast.13, ...), custom_call_target="tpu_custom_call" | custom-call | tf_op jit(solution)/shard_map/triangle_step/pallas_call | solution.py:346
  37.2 0.0 copy-start
  37.2 1.4 %copy.19 = bf16[6,24,128]{2,1,0:T(8,128)(2,1)} copy(bf16[6,24,128]{2,1,0:T(8,128)(2,1)} %bitcast.9) | data formatting | bytes 73728
  38.6 0.0 copy-done
  38.6 0.6 %copy.20 = f32[6,24,128]{2,1,0:T(8,128)} copy(f32[6,24,128]{2,1,0:T(8,128)S(1)} %bitcast.8) | data formatting | bytes 147456
  39.2 0.0 copy-start.2
  39.2 1.7 %copy.21 = f32[128,512]{1,0:T(8,128)} copy(f32[128,512]{1,0:T(8,128)} %get-tuple-element.22) | data formatting | bytes 524288
  40.9 0.0 copy-done.2
  40.9 0.0 copy-start.1
  40.9 0.6 %copy.22 = f32[128,128]{1,0:T(8,128)} copy(f32[128,128]{1,0:T(8,128)S(1)} %copy-done.2) | data formatting | bytes 131072
  41.6 0.2 copy-done.1
  41.8 0.6 %copy.23 = f32[128,128]{1,0:T(8,128)} copy(f32[128,128]{1,0:T(8,128)S(1)} %copy-done.1) | data formatting | bytes 131072
Async XLA Ops:
  37.2 1.4 %copy-start = (f32[144,128]{1,0:T(8,128)S(1)}, f32[144,128]{1,0:T(8,128)}, u32[]{:S(2)}) copy-start(f32[144,128]{1,0:T(8,128)} %get-tuple-element.11) | copy-start | bytes 221188
  39.2 1.7 %copy-start.2 = (f32[128,128]{1,0:T(8,128)S(1)}, f32[128,128]{1,0:T(8,128)}, u32[]{:S(2)}) copy-start(f32[128,128]{1,0:T(8,128)} %get-tuple-element.23) | copy-start | bytes 196612
  40.9 0.9 %copy-start.1 = (f32[128,128]{1,0:T(8,128)S(1)}, f32[128,128]{1,0:T(8,128)}, u32[]{:S(2)}) copy-start(f32[128,128]{1,0:T(8,128)} %get-tuple-element.24) | copy-start | bytes 196612

commit v2 on v1

--- a/solution.py
+++ b/solution.py
@@ -32,10 +32,10 @@
 def kernel(
     R, Q, rows, K, H, C,
     x_ref, cot_ref, ng_ref, nb_ref, pw_ref, gw_ref, tg_ref, tb_ref, ow_ref,
-    out_ref, pg_ref, gp_ref, gg_ref, go_ref,
+    out_ref, pg_ref, gall_ref,
     edges, right32, left32, coef, og_s, hat_s, inv_s, normed_s, dupd_s, dnorm_s,
     tri_s, tri_rcv, d32, drow, drow32, dsend, drecv, dcol32, tnorm_s, dgate_s,
-    g32, gsend, grecv, gfin,
+    gsend, grecv, gfin,
     edge_ss, edge_rs, tri_ss, tri_rs, drow_ss, drow_rs, dcol_ss, dcol_rs,
     gs_ss, gs_rs, gf_ss, gf_rs,
 ):
@@ -71,6 +71,51 @@
         )
 
     loop(1, NP, greet)
+
+    piece = 2 * C // NP
+    per = NP // 2
+
+    def scatter(g, t):
+        other = lax.rem(me + t, NP)
+        return remote(
+            gsend.at[g, other], grecv.at[g, me], gs_ss.at[g, t], gs_rs.at[g, me],
+            other // Q, lax.rem(other, Q),
+        )
+
+    def scatter_start(g, first, second):
+        for p in range(per):
+            gsend[g, p] = first[p * piece : (p + 1) * piece, :].astype(BF16)
+            gsend[g, per + p] = second[p * piece : (p + 1) * piece, :].astype(BF16)
+        loop(1, NP, lambda t: scatter(g, t).start())
+        grecv[g, me] = gsend[g, me]
+
+    def spread(g, t):
+        other = lax.rem(me + t, NP)
+        return remote(
+            gfin.at[g, me], gfin.at[g, me], gf_ss.at[g, t], gf_rs.at[g, me],
+            other // Q, lax.rem(other, Q),
+        )
+
+    def spread_start(g):
+        def wait(t):
+            other = lax.rem(me + NP - t, NP)
+            remote(
+                gsend.at[g, 0], grecv.at[g, other], gs_ss.at[g, t], gs_rs.at[g, other],
+                other // Q, lax.rem(other, Q),
+            ).wait_recv()
+        loop(1, NP, wait)
+        total = grecv[g, 0].astype(F32)
+        for p in range(1, NP):
+            total = total + grecv[g, p].astype(F32)
+        gfin[g, me] = (total / N).astype(BF16)
+        loop(1, NP, lambda t: spread(g, t).start())
+
+    def spread_wait(g, t):
+        other = lax.rem(me + NP - t, NP)
+        remote(
+            gfin.at[g, me], gfin.at[g, other], gf_ss.at[g, t], gf_rs.at[g, other],
+            other // Q, lax.rem(other, Q),
+        ).wait_recv()
 
     hat, inv = normalise(x_ref[...].astype(F32))
     normed = (hat * ng_ref[...] + nb_ref[...]).astype(BF16)
@@ -166,10 +211,10 @@
     for b in range(RPQ):
         parts = []
         for i in range(rows):
-            piece = d32[i * K + b * rows : i * K + (b + 1) * rows, :]
+            block = d32[i * K + b * rows : i * K + (b + 1) * rows, :]
             if pad > rows:
-                piece = jnp.concatenate([piece, jnp.zeros((pad - rows, H), F32)], axis=0)
-            parts.append(piece)
+                block = jnp.concatenate([block, jnp.zeros((pad - rows, H), F32)], axis=0)
+            parts.append(block)
         dsend[b] = jnp.concatenate(parts, axis=0).astype(BF16)
 
     def each_target(act):
@@ -203,8 +248,7 @@
     out_ref[...] = (og * update).astype(BF16)
     d_gate = (cot_ref[...].astype(F32) * update * og * (1.0 - og)).astype(BF16)
     dgate_s[...] = d_gate
-    g32[4 * C : 5 * C, :] = dot(normed_s[...], d_gate, 0, 0)
-    g32[5 * C : 6 * C, :] = dot(tri_norm, dupd_s[...], 0, 0)
+    scatter_start(0, dot(normed_s[...], d_gate, 0, 0), dot(tri_norm, dupd_s[...], 0, 0))
 
     drow32[pl.ds(pl.multiple_of(q * M, 8), M), :] = d_tri32
     for t in range(1, Q):
@@ -227,6 +271,7 @@
         accs = lax.fori_loop(0, K, left_step, accs, unroll=4)
     d_left = jnp.concatenate(accs, axis=0)
     d_proj = [(d_left * coef[0]).astype(BF16), (d_left * coef[1]).astype(BF16)]
+    scatter_start(1, dot(normed_s[...], d_proj[0], 0, 0), dot(normed_s[...], d_proj[1], 0, 0))
 
     edge_wait(1)
 
@@ -259,44 +304,15 @@
     d_right = jnp.concatenate(lax.fori_loop(0, N, right_step, zeros(), unroll=4), axis=0)
     d_proj += [(d_right * coef[2]).astype(BF16), (d_right * coef[3]).astype(BF16)]
 
-    for b in range(4):
-        g32[b * C : (b + 1) * C, :] = dot(normed_s[...], d_proj[b], 0, 0)
-    piece = 6 * C // NP
-    for p in range(NP):
-        gsend[p] = g32[p * piece : (p + 1) * piece, :].astype(BF16)
-
-    def scatter(t):
-        other = lax.rem(me + t, NP)
-        return remote(
-            gsend.at[other], grecv.at[me], gs_ss.at[t], gs_rs.at[me],
-            other // Q, lax.rem(other, Q),
-        )
-    loop(1, NP, lambda t: scatter(t).start())
-    grecv[me] = gsend[me]
+    scatter_start(2, dot(normed_s[...], d_proj[2], 0, 0), dot(normed_s[...], d_proj[3], 0, 0))
+    spread_start(0)
+    spread_start(1)
 
     d_cat = jnp.concatenate(d_proj, axis=-1)
     d_normed = dot(d_cat, pw_ref[...], 1, 1) + dot(dgate_s[...], gw_ref[...], 1, 1)
     pg_ref[...] = norm_back(d_normed * ng_ref[...], hat_s[...], inv_s[...])
 
-    def scatter_wait(t):
-        other = lax.rem(me + NP - t, NP)
-        remote(
-            gsend.at[0], grecv.at[other], gs_ss.at[t], gs_rs.at[other],
-            other // Q, lax.rem(other, Q),
-        ).wait_recv()
-    loop(1, NP, scatter_wait)
-    total = grecv[0].astype(F32)
-    for p in range(1, NP):
-        total = total + grecv[p].astype(F32)
-    gfin[me] = (total / N).astype(BF16)
-
-    def spread(t):
-        other = lax.rem(me + t, NP)
-        return remote(
-            gfin.at[me], gfin.at[me], gf_ss.at[t], gf_rs.at[me],
-            other // Q, lax.rem(other, Q),
-        )
-    loop(1, NP, lambda t: spread(t).start())
+    spread_start(2)
 
     for side in range(2):
         loop(1, R, lambda t, side=side: remote(
@@ -307,22 +323,25 @@
         remote(tri_s.at[other], tri_rcv.at[q], tri_ss.at[t], tri_rs.at[q], r, other).wait_send()
         remote(drow.at[q], drow.at[q], drow_ss.at[t], drow_rs.at[q], r, other).wait_send()
     each_target(lambda b, t, target, other: col_copy(b, t, target, other).wait_send())
-    loop(1, NP, lambda t: scatter(t).wait_send())
-
-    def spread_wait(t):
-        other = lax.rem(me + NP - t, NP)
-        remote(
-            gfin.at[me], gfin.at[other], gf_ss.at[t], gf_rs.at[other],
-            other // Q, lax.rem(other, Q),
-        ).wait_recv()
-    loop(1, NP, spread_wait)
-    for p in range(NP):
-        g32[p * piece : (p + 1) * piece, :] = gfin[p].astype(F32)
-    for b in range(4):
-        gp_ref[:, b * H : (b + 1) * H] = g32[b * C : (b + 1) * C, :]
-    gg_ref[...] = g32[4 * C : 5 * C, :]
-    go_ref[...] = g32[5 * C : 6 * C, :]
-    loop(1, NP, lambda t: spread(t).wait_send())
+    for g in range(3):
+        loop(1, NP, lambda t, g=g: scatter(g, t).wait_send())
+        loop(1, NP, lambda t, g=g: spread_wait(g, t))
+    gall_ref[...] = gfin[...]
+    for g in range(3):
+        loop(1, NP, lambda t, g=g: spread(g, t).wait_send())
+
+
+def finish(NP, piece, C, H, block_ref, grad_ref, gall_ref, out_ref, pg_ref, gp_ref, gg_ref, go_ref):
+    out_ref[...] = block_ref[...]
+    pg_ref[...] = grad_ref[...]
+    targets = (
+        (gg_ref, 0), (go_ref, 0), (gp_ref, 0), (gp_ref, H), (gp_ref, 2 * H), (gp_ref, 3 * H),
+    )
+    per = C // piece
+    for t, (ref, col) in enumerate(targets):
+        for p in range(per):
+            whole = (t % 2) * per + p
+            ref[p * piece : (p + 1) * piece, col : col + H] = gall_ref[t // 2, whole].astype(F32)
 
 
 def local(R, Q, pair_rep, cotangent, ng, nb, pw, gw, tg, tb, ow):
@@ -332,22 +351,20 @@
     NP = R * Q
     RPQ = R // Q
     pad = -(-rows // 8) * 8
-    piece = 6 * C // NP
+    piece = 2 * C // NP
     dma = pltpu.SemaphoreType.DMA
     vmem = pltpu.VMEM
     spec = pl.BlockSpec(memory_space=pltpu.VMEM)
     shapes = (
         jax.ShapeDtypeStruct((M, C), BF16),
         jax.ShapeDtypeStruct((M, C), F32),
-        jax.ShapeDtypeStruct((C, 4 * H), F32),
-        jax.ShapeDtypeStruct((C, C), F32),
-        jax.ShapeDtypeStruct((H, C), F32),
+        jax.ShapeDtypeStruct((3, NP, piece, H), BF16),
     )
-    outs = pl.pallas_call(
+    parts = pl.pallas_call(
         functools.partial(kernel, R, Q, rows, K, H, C),
         out_shape=shapes,
         in_specs=[spec] * 9,
-        out_specs=[spec] * 5,
+        out_specs=[spec] * 3,
         scratch_shapes=[
             vmem((2, R, M, H), BF16),
             vmem((R * M, H), F32),
@@ -369,16 +386,15 @@
             vmem((R * rows * pad, H), F32),
             vmem((M, H), BF16),
             vmem((M, C), BF16),
-            vmem((6 * C, H), F32),
-            vmem((NP, piece, H), BF16),
-            vmem((NP, piece, H), BF16),
-            vmem((NP, piece, H), BF16),
+            vmem((3, NP, piece, H), BF16),
+            vmem((3, NP, piece, H), BF16),
+            vmem((3, NP, piece, H), BF16),
             dma((2, R)), dma((2, R)),
             dma((Q,)), dma((Q,)),
             dma((Q,)), dma((Q,)),
             dma((R,)), dma((R,)),
-            dma((NP,)), dma((NP,)),
-            dma((NP,)), dma((NP,)),
+            dma((3, NP)), dma((3, NP)),
+            dma((3, NP)), dma((3, NP)),
         ],
         compiler_params=pltpu.CompilerParams(
             collective_id=0, has_side_effects=True, vmem_limit_bytes=60 * 1024 * 1024
@@ -388,6 +404,19 @@
         pair_rep.reshape(M, C), cotangent.reshape(M, C), ng.reshape(1, C), nb.reshape(1, C),
         pw, gw, tg.reshape(1, H), tb.reshape(1, H), ow,
     )
+    outs = pl.pallas_call(
+        functools.partial(finish, NP, piece, C, H),
+        out_shape=(
+            shapes[0],
+            shapes[1],
+            jax.ShapeDtypeStruct((C, 4 * H), F32),
+            jax.ShapeDtypeStruct((C, C), F32),
+            jax.ShapeDtypeStruct((H, C), F32),
+        ),
+        in_specs=[spec] * 3,
+        out_specs=[spec] * 5,
+        name="finish",
+    )(*parts)
     return (
         outs[0].reshape(rows, K, C), outs[1].reshape(rows, K, C), outs[2], outs[3], outs[4],
     )

time: 42.7 us -> 39.9 us (0.934)
  local copies, waits for them, and re-layouts: 5.25 us -> 0 us
  Pallas kernels: 36.5 us -> 39.1 us
    unnamed x11 -> x0, local copies, waits for them, and re-layouts: 5.25 us -> none
    pallas_call x0 -> x1, Pallas kernels: none -> 1.78 us  [local(): pl.pallas_call(functools.partial(finish, NP, piece, C, H), out_shape=(sha...]
    pallas_call x1, Pallas kernels: 36.5 us -> 37.3 us  [local(): pl.pallas_call(functools.partial(kernel, R, Q, rows, K, H, C), out_shape=...]
where the time goes in v2:
time: 39.9 us; the launch traced here: 39.7 us
  Pallas kernels  39.1 us (98%)
  between operations  0.64 us (2%)
    pallas_call x1, Pallas kernels, local(): pl.pallas_call(functools.partial(kernel, R, Q, rows, K, H, C), out_shape=...  37.3 us
    pallas_call x1, Pallas kernels, local(): pl.pallas_call(functools.partial(finish, NP, piece, C, H), out_shape=(sha...  1.78 us

profile of v2, /device:TPU:0, one launch (start us, length us, event | category | flops | bytes accessed | tf_op | source)
XLA Modules:
  0.0 39.7 jit_solution(12835262936278890504)
XLA Ops:
  0.6 37.3 %triangle_step.1 = (bf16[144,128]{1,0:T(8,128)(2,1)}, f32[144,128]{1,0:T(8,128)}, bf16[3,16,16,128]{3,2,1,0:T(8,128)(2,1)}) custom-call(bf16[144,128]{1,0:T(8,128)(2,1)} %bitcast.8, bf16[144,128]{1,0:T(8,128)(2,1)} %bitcast.9, f32[1,128]{1,0:T(1,128)} %bitcast.10, f32[1,128]{1,0:T(1,128)} %bitcast.11, bf16[128,512]{1,0:T(8,128)(2,1)} %pw_ref.1, ...), custom_call_target="tpu_custom_call" | custom-call | tf_op jit(solution)/shard_map/triangle_step/pallas_call | solution.py:363
  37.9 1.8 %finish.1 = (bf16[144,128]{1,0:T(8,128)(2,1)}, f32[144,128]{1,0:T(8,128)}, f32[128,512]{1,0:T(8,128)}, f32[128,128]{1,0:T(8,128)}, f32[128,128]{1,0:T(8,128)}) custom-call(bf16[144,128]{1,0:T(8,128)(2,1)} %get-tuple-element.13.block_ref, f32[144,128]{1,0:T(8,128)} %get-tuple-element.14.grad_ref, bf16[3,16,16,128]{3,2,1,0:T(8,128)(2,1)} %get-tuple-element.15.gall_ref), custom_call_target="tpu_custom_call" | custom-call | tf_op jit(solution)/shard_map/finish/pallas_call | solution.py:407

commit v3 on v2

--- a/solution.py
+++ b/solution.py
@@ -55,18 +55,30 @@
         )
 
     def loop(lo, hi, body):
+        if hi - lo <= 16:
+            for t in range(lo, hi):
+                body(t)
+            return
+
         def step(t, carry):
             body(t)
             return carry
-        lax.fori_loop(lo, hi, step, 0, unroll=(hi - lo) <= 16)
+        lax.fori_loop(lo, hi, step, 0)
+
+    def wrap(value, size):
+        return jnp.where(value >= size, value - size, value)
+
+    def peer(t):
+        rr, qq = wrap(r + t // Q, R), wrap(q + t % Q, Q)
+        return rr, qq, rr * Q + qq
 
     barrier = pltpu.get_barrier_semaphore()
 
     def greet(t):
-        other = lax.rem(me + t, NP)
+        rr, qq, _ = peer(t)
         pl.semaphore_signal(
             barrier, inc=1,
-            device_id={"row": other // Q, "col": lax.rem(other, Q)},
+            device_id={"row": rr, "col": qq},
             device_id_type=pl.DeviceIdType.MESH,
         )
 
@@ -76,10 +88,15 @@
     per = NP // 2
 
     def scatter(g, t):
-        other = lax.rem(me + t, NP)
+        rr, qq, other = peer(t)
         return remote(
-            gsend.at[g, other], grecv.at[g, me], gs_ss.at[g, t], gs_rs.at[g, me],
-            other // Q, lax.rem(other, Q),
+            gsend.at[g, other], grecv.at[g, me], gs_ss.at[g], gs_rs.at[g], rr, qq
+        )
+
+    def scatter_all(g):
+        block = pl.ds(0, NP - 1)
+        return remote(
+            gsend.at[g, block], grecv.at[g, block], gs_ss.at[g], gs_rs.at[g], r, q
         )
 
     def scatter_start(g, first, second):
@@ -90,32 +107,20 @@
         grecv[g, me] = gsend[g, me]
 
     def spread(g, t):
-        other = lax.rem(me + t, NP)
-        return remote(
-            gfin.at[g, me], gfin.at[g, me], gf_ss.at[g, t], gf_rs.at[g, me],
-            other // Q, lax.rem(other, Q),
-        )
+        rr, qq, _ = peer(t)
+        return remote(gfin.at[g, me], gfin.at[g, me], gf_ss.at[g], gf_rs.at[g], rr, qq)
+
+    def spread_all(g):
+        block = pl.ds(0, NP - 1)
+        return remote(gfin.at[g, block], gfin.at[g, block], gf_ss.at[g], gf_rs.at[g], r, q)
 
     def spread_start(g):
-        def wait(t):
-            other = lax.rem(me + NP - t, NP)
-            remote(
-                gsend.at[g, 0], grecv.at[g, other], gs_ss.at[g, t], gs_rs.at[g, other],
-                other // Q, lax.rem(other, Q),
-            ).wait_recv()
-        loop(1, NP, wait)
+        scatter_all(g).wait_recv()
         total = grecv[g, 0].astype(F32)
         for p in range(1, NP):
             total = total + grecv[g, p].astype(F32)
         gfin[g, me] = (total / N).astype(BF16)
         loop(1, NP, lambda t: spread(g, t).start())
-
-    def spread_wait(g, t):
-        other = lax.rem(me + NP - t, NP)
-        remote(
-            gfin.at[g, me], gfin.at[g, other], gf_ss.at[g, t], gf_rs.at[g, other],
-            other // Q, lax.rem(other, Q),
-        ).wait_recv()
 
     hat, inv = normalise(x_ref[...].astype(F32))
     normed = (hat * ng_ref[...] + nb_ref[...]).astype(BF16)
@@ -135,23 +140,58 @@
 
     pl.semaphore_wait(barrier, NP - 1)
 
-    for side in range(2):
-        def send(t, side=side):
-            other = lax.rem(r + t, R)
+    B = 2 if R % 2 == 0 else 1
+    A = R // B
+    place, lane = r // B, lax.rem(r, B)
+
+    def along(act):
+        for d in range(1, A):
+            for spot in (place - d, place + d):
+                @pl.when(jnp.logical_and(spot >= 0, spot < A))
+                def _(spot=spot):
+                    act(jnp.clip(spot, 0, A - 1))
+
+    def line_copy(side, spot):
+        return remote(
+            edges.at[side, r], edges.at[side, r], edge_ss.at[side, spot],
+            edge_rs.at[side, r], spot * B + lane, q,
+        )
+
+    def lane_copy(side, spot):
+        slot = spot * B + lane
+        return remote(
+            edges.at[side, slot], edges.at[side, slot], edge_ss.at[side, A + spot],
+            edge_rs.at[side, slot], place * B + (B - 1 - lane), q,
+        )
+
+    def edge_send(side):
+        along(lambda spot: line_copy(side, spot).start())
+        if B > 1:
+            lane_copy(side, place).start()
+
+    def edge_pass(side):
+        def one(spot):
+            slot = spot * B + lane
             remote(
-                edges.at[side, r], edges.at[side, r], edge_ss.at[side, t], edge_rs.at[side, r],
-                other, q,
-            ).start()
-        loop(1, R, send)
+                edges.at[side, r], edges.at[side, slot], edge_ss.at[side, 0],
+                edge_rs.at[side, slot], slot, q,
+            ).wait_recv()
+            if B > 1:
+                lane_copy(side, spot).start()
+        along(one)
 
     def edge_wait(side):
-        def wait(t):
-            other = lax.rem(r + R - t, R)
-            remote(
-                edges.at[side, r], edges.at[side, other], edge_ss.at[side, t],
-                edge_rs.at[side, other], other, q,
-            ).wait_recv()
-        loop(1, R, wait)
+        if B > 1:
+            def wait(spot):
+                slot = spot * B + (B - 1 - lane)
+                remote(
+                    edges.at[side, r], edges.at[side, slot], edge_ss.at[side, 0],
+                    edge_rs.at[side, slot], place * B + (B - 1 - lane), q,
+                ).wait_recv()
+            loop(0, A, wait)
+
+    edge_send(0)
+    edge_send(1)
 
     own = pl.multiple_of(r * M, 8)
     left32[pl.ds(own, M), :] = left_edge.astype(F32)
@@ -165,6 +205,7 @@
     dupd_s[...] = d_update
     dnorm_s[...] = dot(d_update, ow_ref[...], 1, 1) * tg_ref[...]
 
+    edge_pass(0)
     edge_wait(0)
 
     def widen_right(t):
@@ -186,15 +227,16 @@
             tri_s[half, i * K : (i + 1) * K, :] = accs[i]
 
     for t in range(1, Q):
-        other = lax.rem(q + t, Q)
+        other = wrap(q + t, Q)
         partial(other)
         remote(
             tri_s.at[other], tri_rcv.at[q], tri_ss.at[t], tri_rs.at[q], r, other
         ).start()
     partial(q)
+    edge_pass(1)
     triangle = tri_s[q]
     for t in range(1, Q):
-        other = lax.rem(q + Q - t, Q)
+        other = wrap(q + Q - t, Q)
         remote(
             tri_s.at[other], tri_rcv.at[other], tri_ss.at[t], tri_rs.at[other], r, other
         ).wait_recv()
@@ -204,7 +246,7 @@
     d_tri = norm_back(dnorm_s[...], tri_hat, tri_inv).astype(BF16)
     drow[q] = d_tri
     for t in range(1, Q):
-        other = lax.rem(q + t, Q)
+        other = wrap(q + t, Q)
         remote(drow.at[q], drow.at[q], drow_ss.at[t], drow_rs.at[q], r, other).start()
     d_tri32 = d_tri.astype(F32)
     d32[...] = d_tri32
@@ -221,7 +263,7 @@
         for t in range(Q):
             def one(b, t=t):
                 target = q * RPQ + b
-                other = lax.rem(q + t, Q)
+                other = wrap(q + t, Q)
                 if t:
                     act(b, t, target, other)
                 else:
@@ -252,7 +294,7 @@
 
     drow32[pl.ds(pl.multiple_of(q * M, 8), M), :] = d_tri32
     for t in range(1, Q):
-        other = lax.rem(q + Q - t, Q)
+        other = wrap(q + Q - t, Q)
         remote(
             drow.at[q], drow.at[other], drow_ss.at[t], drow_rs.at[other], r, other
         ).wait_recv()
@@ -271,7 +313,8 @@
         accs = lax.fori_loop(0, K, left_step, accs, unroll=4)
     d_left = jnp.concatenate(accs, axis=0)
     d_proj = [(d_left * coef[0]).astype(BF16), (d_left * coef[1]).astype(BF16)]
-    scatter_start(1, dot(normed_s[...], d_proj[0], 0, 0), dot(normed_s[...], d_proj[1], 0, 0))
+    wide = dot(normed_s[...], jnp.concatenate(d_proj, axis=-1), 0, 0)
+    scatter_start(1, wide[:, :H], wide[:, H:])
 
     edge_wait(1)
 
@@ -282,7 +325,7 @@
     owner = r // RPQ
 
     def col_wait(t):
-        source = lax.rem(r + R - t, R)
+        source = wrap(r + R - t, R)
         remote(
             dsend.at[0], drecv.at[source], dcol_ss.at[0], dcol_rs.at[source], source, owner
         ).wait_recv()
@@ -304,7 +347,8 @@
     d_right = jnp.concatenate(lax.fori_loop(0, N, right_step, zeros(), unroll=4), axis=0)
     d_proj += [(d_right * coef[2]).astype(BF16), (d_right * coef[3]).astype(BF16)]
 
-    scatter_start(2, dot(normed_s[...], d_proj[2], 0, 0), dot(normed_s[...], d_proj[3], 0, 0))
+    wide = dot(normed_s[...], jnp.concatenate(d_proj[2:], axis=-1), 0, 0)
+    scatter_start(2, wide[:, :H], wide[:, H:])
     spread_start(0)
     spread_start(1)
 
@@ -315,20 +359,20 @@
     spread_start(2)
 
     for side in range(2):
-        loop(1, R, lambda t, side=side: remote(
-            edges.at[side, r], edges.at[side, r], edge_ss.at[side, t], edge_rs.at[side, r], r, q
-        ).wait_send())
+        along(lambda spot, side=side: line_copy(side, spot).wait_send())
+        if B > 1:
+            loop(0, A, lambda spot, side=side: lane_copy(side, spot).wait_send())
     for t in range(1, Q):
-        other = lax.rem(q + t, Q)
+        other = wrap(q + t, Q)
         remote(tri_s.at[other], tri_rcv.at[q], tri_ss.at[t], tri_rs.at[q], r, other).wait_send()
         remote(drow.at[q], drow.at[q], drow_ss.at[t], drow_rs.at[q], r, other).wait_send()
     each_target(lambda b, t, target, other: col_copy(b, t, target, other).wait_send())
     for g in range(3):
-        loop(1, NP, lambda t, g=g: scatter(g, t).wait_send())
-        loop(1, NP, lambda t, g=g: spread_wait(g, t))
+        scatter_all(g).wait_send()
+        spread_all(g).wait_recv()
     gall_ref[...] = gfin[...]
     for g in range(3):
-        loop(1, NP, lambda t, g=g: spread(g, t).wait_send())
+        spread_all(g).wait_send()
 
 
 def finish(NP, piece, C, H, block_ref, grad_ref, gall_ref, out_ref, pg_ref, gp_ref, gg_ref, go_ref):
@@ -389,12 +433,12 @@
             vmem((3, NP, piece, H), BF16),
             vmem((3, NP, piece, H), BF16),
             vmem((3, NP, piece, H), BF16),
-            dma((2, R)), dma((2, R)),
+            dma((2, 2 * R)), dma((2, R)),
             dma((Q,)), dma((Q,)),
             dma((Q,)), dma((Q,)),
             dma((R,)), dma((R,)),
-            dma((3, NP)), dma((3, NP)),
-            dma((3, NP)), dma((3, NP)),
+            dma((3,)), dma((3,)),
+            dma((3,)), dma((3,)),
         ],
         compiler_params=pltpu.CompilerParams(
             collective_id=0, has_side_effects=True, vmem_limit_bytes=60 * 1024 * 1024

time: 39.9 us -> 36.6 us (0.917)
  Pallas kernels: 39.1 us -> 35.8 us
    pallas_call x1, Pallas kernels: 37.3 us -> 34.1 us  [local(): pl.pallas_call(functools.partial(kernel, R, Q, rows, K, H, C), out_shape=...]
where the time goes in v3:
time: 36.6 us; the launch traced here: 36.5 us
  Pallas kernels  35.8 us (98%)
  between operations  0.64 us (2%)
    pallas_call x1, Pallas kernels, local(): pl.pallas_call(functools.partial(kernel, R, Q, rows, K, H, C), out_shape=...  34.1 us
    pallas_call x1, Pallas kernels, local(): pl.pallas_call(functools.partial(finish, NP, piece, C, H), out_shape=(sha...  1.78 us

profile of v3, /device:TPU:0, one launch (start us, length us, event | category | flops | bytes accessed | tf_op | source)
XLA Modules:
  0.0 36.5 jit_solution(5042667939800507855)
XLA Ops:
  0.6 34.1 %triangle_step.1 = (bf16[144,128]{1,0:T(8,128)(2,1)}, f32[144,128]{1,0:T(8,128)}, bf16[3,16,16,128]{3,2,1,0:T(8,128)(2,1)}) custom-call(bf16[144,128]{1,0:T(8,128)(2,1)} %bitcast.8, bf16[144,128]{1,0:T(8,128)(2,1)} %bitcast.9, f32[1,128]{1,0:T(1,128)} %bitcast.10, f32[1,128]{1,0:T(1,128)} %bitcast.11, bf16[128,512]{1,0:T(8,128)(2,1)} %pw_ref.1, ...), custom_call_target="tpu_custom_call" | custom-call | tf_op jit(solution)/shard_map/triangle_step/pallas_call | solution.py:407
  34.7 1.8 %finish.1 = (bf16[144,128]{1,0:T(8,128)(2,1)}, f32[144,128]{1,0:T(8,128)}, f32[128,512]{1,0:T(8,128)}, f32[128,128]{1,0:T(8,128)}, f32[128,128]{1,0:T(8,128)}) custom-call(bf16[144,128]{1,0:T(8,128)(2,1)} %get-tuple-element.13.block_ref, f32[144,128]{1,0:T(8,128)} %get-tuple-element.14.grad_ref, bf16[3,16,16,128]{3,2,1,0:T(8,128)(2,1)} %get-tuple-element.15.gall_ref), custom_call_target="tpu_custom_call" | custom-call | tf_op jit(solution)/shard_map/finish/pallas_call | solution.py:451

commit v4 on v3

--- a/solution.py
+++ b/solution.py
@@ -191,7 +191,6 @@
             loop(0, A, wait)
 
     edge_send(0)
-    edge_send(1)
 
     own = pl.multiple_of(r * M, 8)
     left32[pl.ds(own, M), :] = left_edge.astype(F32)
@@ -206,6 +205,7 @@
     dnorm_s[...] = dot(d_update, ow_ref[...], 1, 1) * tg_ref[...]
 
     edge_pass(0)
+    edge_send(1)
     edge_wait(0)
 
     def widen_right(t):
@@ -290,7 +290,6 @@
     out_ref[...] = (og * update).astype(BF16)
     d_gate = (cot_ref[...].astype(F32) * update * og * (1.0 - og)).astype(BF16)
     dgate_s[...] = d_gate
-    scatter_start(0, dot(normed_s[...], d_gate, 0, 0), dot(tri_norm, dupd_s[...], 0, 0))
 
     drow32[pl.ds(pl.multiple_of(q * M, 8), M), :] = d_tri32
     for t in range(1, Q):
@@ -316,6 +315,7 @@
     wide = dot(normed_s[...], jnp.concatenate(d_proj, axis=-1), 0, 0)
     scatter_start(1, wide[:, :H], wide[:, H:])
 
+    scatter_start(0, dot(normed_s[...], d_gate, 0, 0), dot(tri_norm, dupd_s[...], 0, 0))
     edge_wait(1)
 
     def widen_left(t):

time: 36.6 us -> 34.2 us (0.934)
  Pallas kernels: 35.8 us -> 33.4 us
    pallas_call x1, Pallas kernels: 34.1 us -> 31.6 us  [local(): pl.pallas_call(functools.partial(kernel, R, Q, rows, K, H, C), out_shape=...]
where the time goes in v4:
time: 34.2 us; the launch traced here: 34 us
  Pallas kernels  33.4 us (98%)
  between operations  0.64 us (2%)
    pallas_call x1, Pallas kernels, local(): pl.pallas_call(functools.partial(kernel, R, Q, rows, K, H, C), out_shape=...  31.6 us
    pallas_call x1, Pallas kernels, local(): pl.pallas_call(functools.partial(finish, NP, piece, C, H), out_shape=(sha...  1.78 us

profile of v4, /device:TPU:0, one launch (start us, length us, event | category | flops | bytes accessed | tf_op | source)
XLA Modules:
  0.0 34.0 jit_solution(17206618748226997181)
XLA Ops:
  0.6 31.6 %triangle_step.1 = (bf16[144,128]{1,0:T(8,128)(2,1)}, f32[144,128]{1,0:T(8,128)}, bf16[3,16,16,128]{3,2,1,0:T(8,128)(2,1)}) custom-call(bf16[144,128]{1,0:T(8,128)(2,1)} %bitcast.8, bf16[144,128]{1,0:T(8,128)(2,1)} %bitcast.9, f32[1,128]{1,0:T(1,128)} %bitcast.10, f32[1,128]{1,0:T(1,128)} %bitcast.11, bf16[128,512]{1,0:T(8,128)(2,1)} %pw_ref.1, ...), custom_call_target="tpu_custom_call" | custom-call | tf_op jit(solution)/shard_map/triangle_step/pallas_call | solution.py:407
  32.2 1.8 %finish.1 = (bf16[144,128]{1,0:T(8,128)(2,1)}, f32[144,128]{1,0:T(8,128)}, f32[128,512]{1,0:T(8,128)}, f32[128,128]{1,0:T(8,128)}, f32[128,128]{1,0:T(8,128)}) custom-call(bf16[144,128]{1,0:T(8,128)(2,1)} %get-tuple-element.13.block_ref, f32[144,128]{1,0:T(8,128)} %get-tuple-element.14.grad_ref, bf16[3,16,16,128]{3,2,1,0:T(8,128)(2,1)} %get-tuple-element.15.gall_ref), custom_call_target="tpu_custom_call" | custom-call | tf_op jit(solution)/shard_map/finish/pallas_call | solution.py:451
